TPU v7x, 32 devices: a whole 2x2x4 slice. The times are simulated.
32 devices in a mesh: ctx: 8 (over y, x, core), head: 4 (over z).
Axes of the slice: x: 2, y: 2, z: 4, core: 2. Of those that a mesh axis runs over, the one named last changes fastest.
Arguments:
- block_order: int32 [16], replicated, may hold values from 0 to 15, as said below
- query_latent: bfloat16 [1024, 128, 576], P('ctx', 'head'), may hold values from -12 to 12
- key_latent: bfloat16 [1024, 576], P('ctx'), may hold values from -6 to 6
- normalizer: float32 [1024, 128], P('ctx', 'head'), may hold values from 6 to 9
- indexer_query: bfloat16 [1024, 64, 128], P('ctx', 'head'), may hold values from -8 to 8
- indexer_key: bfloat16 [1024, 128], P('ctx'), may hold values from -4 to 4
- indexer_weight: bfloat16 [1024, 64], P('ctx', 'head'), may hold values from -4 to 4
Outputs:
- query_grad: float32 [1024, 64, 128], P('ctx', 'head')
- key_grad: float32 [1024, 128], P(('ctx', 'head'))
Inputs may be any that keep to these rules, and one draw needn't show every extreme that they name: `block_order`: entries 2 i and 2 i + 1 are the blocks stored on ctx index i; all entries together are each of 0 to 15 once, and the two entries of one index sum to 15.
All inputs are finite; a program needn't handle non-finite values.
Results may differ from a plain program's by a relative error of at most 0.0037.
Values may be sent and summed in bfloat16 or wider, within the bound.
A program may use at most 128 MiB of HBM per device.

v0:
```python
import math
import jax
import jax.numpy as jnp
from jax import lax
from jax.sharding import PartitionSpec as P

mla_scale = 192.0 ** (-0.5)
loss_scale = 64.0


def gradient(tile_sums, query_pos, key_pos):
    visible = key_pos[None, :] <= query_pos[:, None]
    target_sum = jnp.where(visible, tile_sums[0], 0.0)
    row_total = jnp.sum(target_sum, axis=1, keepdims=True)
    logits = tile_sums[1]
    row_top = jnp.max(jnp.where(visible, logits, -jnp.inf), axis=1, keepdims=True)
    exp_logit = jnp.where(visible, jnp.exp(logits - row_top), 0.0)
    norm_sum = jnp.sum(exp_logit, axis=1, keepdims=True)
    return jnp.where(
        visible, loss_scale * (exp_logit / norm_sum - target_sum / row_total), 0.0
    ).astype(jnp.bfloat16)


def per_device(
    block_order, query_latent, key_latent, normalizer, indexer_query, indexer_key, indexer_weight
):
    query_rows = query_latent.shape[0]
    block_rows = query_rows // 2
    cycle_count = lax.axis_size("ctx")
    group_count = lax.axis_size("head")
    tokens = query_rows * cycle_count
    local_heads = indexer_query.shape[1]
    idx_scale = (local_heads * group_count * indexer_query.shape[2]) ** (-0.5)
    key_pos = (
        block_order[:, None] * block_rows + jnp.arange(block_rows, dtype=jnp.int32)[None, :]
    ).reshape(-1)
    query_pos = lax.dynamic_slice_in_dim(key_pos, lax.axis_index("ctx") * query_rows, query_rows, 0)
    all_latent, all_index = (
        lax.all_gather(key_latent, "ctx", axis=0, tiled=True),
        lax.all_gather(indexer_key, "ctx", axis=0, tiled=True),
    )
    key_block = math.gcd(tokens, 512)
    block_count = tokens // key_block
    weight_float = indexer_weight.astype(jnp.float32)

    def forward(step_index, state):
        tile_sums, positive = state
        offset = step_index * key_block
        latent_block = lax.dynamic_slice_in_dim(all_latent, offset, key_block, 0)
        index_block = lax.dynamic_slice_in_dim(all_index, offset, key_block, 0)
        scores = (
            jnp.einsum(
                "thl,sl->ths", query_latent, latent_block, preferred_element_type=jnp.float32
            )
            * mla_scale
        )
        target_part = jnp.sum(jnp.exp(scores - normalizer[:, :, None]), axis=1)
        idx_dot = jnp.einsum(
            "tjd,sd->tjs", indexer_query, index_block, preferred_element_type=jnp.float32
        )
        logit_part = idx_scale * jnp.sum(
            weight_float[:, :, None] * jnp.maximum(idx_dot, 0.0), axis=1
        )
        tile_sums = lax.dynamic_update_slice_in_dim(
            tile_sums, jnp.stack((target_part, logit_part)), offset, 2
        )
        positive = lax.dynamic_update_slice_in_dim(positive, idx_dot > 0, offset, 2)
        return (tile_sums, positive)

    start_state = (
        jnp.zeros((2, query_rows, tokens), jnp.float32),
        jnp.zeros((query_rows, local_heads, tokens), jnp.bool_),
    )
    tile_sums, positive = lax.fori_loop(0, block_count, forward, start_state)
    share_sums = lax.psum_scatter(tile_sums, "head", scatter_dimension=1, tiled=True)
    share_count = query_rows // group_count
    share_pos = lax.dynamic_slice_in_dim(
        query_pos, lax.axis_index("head") * share_count, share_count, 0
    )
    share_grad = gradient(share_sums, share_pos, key_pos)
    grad_logit = lax.all_gather(share_grad, "head", axis=0, tiled=True)
    weight_scaled = weight_float * idx_scale

    def backward(step_index, state):
        coeff_buffer, query_accum = state
        offset = step_index * key_block
        positive_block = lax.dynamic_slice_in_dim(positive, offset, key_block, 2)
        grad_block = lax.dynamic_slice_in_dim(grad_logit, offset, key_block, 1)
        coeff_block = jnp.where(
            positive_block,
            grad_block.astype(jnp.float32)[:, None, :] * weight_scaled[:, :, None],
            0.0,
        ).astype(jnp.bfloat16)
        index_block = lax.dynamic_slice_in_dim(all_index, offset, key_block, 0)
        query_accum = query_accum + jnp.einsum(
            "tjs,sd->tjd", coeff_block, index_block, preferred_element_type=jnp.float32
        )
        coeff_buffer = lax.dynamic_update_slice_in_dim(coeff_buffer, coeff_block, offset, 2)
        return (coeff_buffer, query_accum)

    back_state = (
        jnp.zeros((query_rows, local_heads, tokens), jnp.bfloat16),
        jnp.zeros(indexer_query.shape, jnp.float32),
    )
    coefficient, query_grad = lax.fori_loop(0, block_count, backward, back_state)
    key_grad = lax.psum_scatter(
        jnp.einsum("tjs,tjd->sd", coefficient, indexer_query, preferred_element_type=jnp.float32),
        ("ctx", "head"),
        scatter_dimension=0,
        tiled=True,
    )
    return (query_grad, key_grad)


def solution(mesh):
    return jax.shard_map(
        per_device,
        mesh=mesh,
        in_specs=(
            P(),
            P("ctx", "head", None),
            P("ctx", None),
            P("ctx", "head"),
            P("ctx", "head", None),
            P("ctx", None),
            P("ctx", "head"),
        ),
        out_specs=(P("ctx", "head", None), P(("ctx", "head"), None)),
        check_vma=False,
    )
```

profile of v0, /device:TPU:0, one launch (start us, length us, event | category | flops | bytes accessed | tf_op | source)
XLA Modules:
  0.0 269.6 jit_solution(7283531578134878488)
XLA Ops:
  7.2 0.0 all-gather.2.cloned.1.call-start
  7.2 0.7 all-gather.2.cloned.1.call-update
  7.9 0.0 reduce-scatter.3.cloned.1.call-start
  8.0 0.7 convert_element_type.20
  8.6 1.2 copy.14
  9.8 11.0 %all_gather.10 = bf16[1024,128]{1,0:T(8,128)(2,1)S(1)} all-gather(bf16[128,128]{1,0:T(8,128)(2,1)} %param.16), channel_id=1, replica_groups=mesh['ctx'=8,'head'=4] {'ctx'}, dimensions={0}, use_global_device_ids=true | all-gather | bytes 294912 | tf_op jit(solution)/shard_map/all_gather | solution.py:40
  20.8 15.8 %all-gather.2.cloned.1.call-done = bf16[1024,576]{0,1:T(8,128)(2,1)} async-done(((bf16[128,576]{0,1:T(8,128)(2,1)}), bf16[1024,576]{0,1:T(8,128)(2,1)}) %all-gather.2.cloned.1.call-update) | async-done | bytes 1179664 | tf_op jit(solution)/shard_map/all_gather | solution.py:39
  36.7 1.1 broadcast_in_dim.49.clone
  37.8 0.8 broadcast_in_dim.50
  38.6 0.0 copy-done.9
  38.6 0.0 copy-start.10
  38.6 0.0 copy-start.8
  38.6 27.1 %while.31 = (s32[]{:T(128)}, f32[2,128,1024]{2,1,0:T(8,128)}, pred[128,16,1024]{0,2,1:T(32,128)(4,1)S(1)}, bf16[1024,576]{0,1:T(8,128)(2,1)}, bf16[128,32,576]{0...) while((s32[]{:T(128)}, f32[2,128,1024]{2,1,0:T(8,128)}, ...), condition=%wide.region_3.0_spmd, body=%wide.region_0.0_spmd.sunk | while | flops 2694905856 | bytes 23814388 | solution.py:74
  38.6 0.0 copy-start
  38.7 6.8 %exponential_reduce_fusion.2 = f32[512,128]{1,0:T(8,128)S(1)} fusion(f32[128,32]{0,1:T(8,128)S(1)} %get-tuple-element.515, bf16[128,32,576]{0,2,1:T(8,128)(2,1)} %get-tuple-element.514, bf16[1024,576]{0,1:T(8,128)(2,1)} %get-tuple-element.513, s32[]{:T(128)S(6)} %select_n.87), kind=kOutput, calls=%fused_computation.clone.1 | convolution fusion | flops 2422145024 | bytes 5586948 | tf_op jit(solution)/shard_map/while/body/eval_jaxpr/thl,sl->ths/dot_general | solution.py:52
  45.5 0.0 copy-done
  45.5 2.7 multiply_reduce_fusion.2
  48.2 0.1 pad_maximum_fusion.2
  48.2 0.2 copy.30
  48.4 0.0 copy-start.1
  48.4 0.9 constant_dynamic-update-slice_fusion.2
  49.3 2.8 %bitcast_dynamic-update-slice_fusion.2 = pred[128,16,1024]{0,2,1:T(32,128)(4,1)S(1)} fusion(pred[128,16,1024]{0,2,1:T(32,128)(4,1)S(1)} %get-tuple-element.499, s32[]{:T(128)S(6)} %select_n.87, f32[512,128,16]{1,0,2:T(8,128)} %get-tuple-element.476), kind=kLoop, calls=%fused_computation.2.clone.1 | loop fusion | flops 1048576 | bytes 5242884 | tf_op jit(solution)/shard_map/while/body/eval_jaxpr/dynamic_update_slice | solution.py:67
  52.2 0.0 copy-start
  52.2 6.8 %exponential_reduce_fusion.2 = f32[512,128]{1,0:T(8,128)S(1)} fusion(f32[128,32]{0,1:T(8,128)S(1)} %get-tuple-element.515, bf16[128,32,576]{0,2,1:T(8,128)(2,1)} %get-tuple-element.514, bf16[1024,576]{0,1:T(8,128)(2,1)} %get-tuple-element.513, s32[]{:T(128)S(6)} %select_n.87), kind=kOutput, calls=%fused_computation.clone.1 | convolution fusion | flops 2422145024 | bytes 5586948 | tf_op jit(solution)/shard_map/while/body/eval_jaxpr/thl,sl->ths/dot_general | solution.py:52
  59.0 2.7 multiply_reduce_fusion.2
  61.7 0.1 pad_maximum_fusion.2
  61.8 0.2 copy.30
  62.0 0.0 copy-start.1
  62.0 0.9 constant_dynamic-update-slice_fusion.2
  62.9 2.8 %bitcast_dynamic-update-slice_fusion.2 = pred[128,16,1024]{0,2,1:T(32,128)(4,1)S(1)} fusion(pred[128,16,1024]{0,2,1:T(32,128)(4,1)S(1)} %get-tuple-element.499, s32[]{:T(128)S(6)} %select_n.87, f32[512,128,16]{1,0,2:T(8,128)} %get-tuple-element.476), kind=kLoop, calls=%fused_computation.2.clone.1 | loop fusion | flops 1048576 | bytes 5242884 | tf_op jit(solution)/shard_map/while/body/eval_jaxpr/dynamic_update_slice | solution.py:67
  65.7 0.0 reduce-scatter.3.cloned.1.call-update
  65.8 0.0 reduce-scatter.5.cloned.1.call-start
  65.8 0.1 iota_add_fusion
  65.9 0.1 add.94
  66.0 0.1 dynamic_slice.42
  66.1 0.0 copy-done.8
  66.1 27.1 %reduce-scatter.3.cloned.1.call-done = f32[2,32,1024]{2,1,0:T(8,128)} async-done(((f32[2,128,1024]{2,1,0:T(8,128)}), f32[2,32,1024]{2,1,0:T(8,128)}) %reduce-scatter.3.cloned.1.call-update) | async-done | bytes 262160 | tf_op jit(solution)/shard_map/reduce_scatter | solution.py:75
  93.2 1.1 fusion.17
  94.3 1.2 fusion.20
  95.5 1.1 fusion.18
  96.6 14.5 %all_gather.11 = bf16[128,1024]{1,0:T(8,128)(2,1)S(1)} all-gather(bf16[32,1024]{1,0:T(8,128)(2,1)S(1)} %fusion.18), channel_id=1, replica_groups=mesh['ctx'=8,'head'=4] {'head'}, dimensions={0}, use_global_device_ids=true | all-gather | bytes 327680 | tf_op jit(solution)/shard_map/all_gather | solution.py:81
  111.0 2.5 broadcast_in_dim.47
  113.5 10.9 %while.32 = (s32[]{:T(128)}, bf16[128,16,1024]{2,0,1:T(8,128)(2,1)}, f32[128,16,128]{2,0,1:T(8,128)}, pred[128,16,1024]{0,2,1:T(32,128)(4,1)S(1)}, bf16[128,1024...) while((s32[]{:T(128)}, ...), condition=%wide.region_9.10_spmd.clone, body=%wide.region_8.9_spmd.clone.sunk | while | flops 275316736 | bytes 53494056 | solution.py:105
  113.6 0.0 copy-start.2
  113.6 0.1 constant_dynamic-slice_fusion.2
  113.6 1.2 copy.31
  114.9 0.0 copy-done.4
  114.9 1.0 fusion.36
  115.9 0.2 copy-done.2
  116.1 0.7 fusion.35
  116.8 0.3 copy-done.5
  117.1 1.9 copy-done.3
  119.0 0.1 constant_dynamic-slice_fusion.2
  119.1 1.2 copy.31
  120.3 0.0 copy-done.4
  120.4 1.0 fusion.36
  121.4 0.1 copy-done.2
  121.5 0.7 fusion.35
  122.2 0.3 copy-done.5
  122.5 1.9 copy-done.3
  124.4 4.4 %convolution_bitcast_fusion = f32[1024,128]{1,0:T(8,128)} fusion(bf16[128,16,1024]{2,0,1:T(8,128)(2,1)} %get-tuple-element.285, bf16[128,16,128]{2,1,0:T(8,128)(2,1)S(1)} %copy-done.7), kind=kOutput, calls=%fused_computation.26 | convolution fusion | flops 536870912 | bytes 5242880 | tf_op jit(solution)/shard_map/tjs,tjd->sd/dot_general | solution.py:107
  128.8 0.0 reduce-scatter.5.cloned.1.call-update
  128.8 1.6 copy.19
  130.4 132.7 %reduce-scatter.5.cloned.1.call-done = f32[32,128]{1,0:T(8,128)} async-done(((f32[1024,128]{1,0:T(8,128)}), f32[32,128]{1,0:T(8,128)}) %reduce-scatter.5.cloned.1.call-update) | async-done | bytes 16400 | tf_op jit(solution)/shard_map/reduce_scatter | solution.py:106
  (23 shorter events, 0.1 us)
Async XLA Ops:
  7.2 31.4 %copy-start.9 = (f32[128,32]{0,1:T(8,128)S(1)}, f32[128,32]{0,1:T(8,128)}, u32[]{:S(2)}) copy-start(f32[128,32]{0,1:T(8,128)} %param.14) | copy-start | bytes 49156
  7.2 29.5 %all-gather.2.cloned.1.call-start = ((), (), s32[]{:S(2)}) async-start(), calls=%async_computation.2 | async-start | bytes 1327104 | tf_op jit(solution)/shard_map/all_gather | solution.py:39
  7.9 85.3 %reduce-scatter.3.cloned.1.call-start = ((), (), s32[]{:S(2)}) async-start(), calls=%async_computation.3 | async-start | bytes 1310720 | tf_op jit(solution)/shard_map/reduce_scatter | solution.py:75
  38.6 27.2 %copy-start.10 = (s32[16]{0:T(128)S(1)}, s32[16]{0:T(128)}, u32[]{:S(2)}) copy-start(s32[16]{0:T(128)} %param.11) | copy-start | bytes 196
  38.6 27.5 %copy-start.8 = (bf16[128,16]{0,1:T(8,128)(2,1)S(1)}, bf16[128,16]{0,1:T(8,128)(2,1)}, u32[]{:S(2)}) copy-start(bf16[128,16]{0,1:T(8,128)(2,1)} %param.17) | copy-start | bytes 12292
  38.6 6.8 %copy-start = (bf16[128,16,128]{2,0,1:T(8,128)(2,1)}, bf16[128,16,128]{2,0,1:T(8,128)(2,1)S(1)}, u32[]{:S(2)}) copy-start(bf16[128,16,128]{2,0,1:T(8,128)(2,1)S(1)} %get-tuple-element.518) | copy-start | bytes 1572868 | tf_op jit(solution)/shard_map/while
  48.4 3.7 %copy-start.1 = (bf16[128,16,128]{2,0,1:T(8,128)(2,1)S(1)}, bf16[128,16,128]{2,0,1:T(8,128)(2,1)}, u32[]{:S(2)}) copy-start(bf16[128,16,128]{2,0,1:T(8,128)(2,1)} %copy-done) | copy-start | bytes 1572868 | tf_op jit(solution)/shard_map/while
  52.2 6.8 %copy-start = (bf16[128,16,128]{2,0,1:T(8,128)(2,1)}, bf16[128,16,128]{2,0,1:T(8,128)(2,1)S(1)}, u32[]{:S(2)}) copy-start(bf16[128,16,128]{2,0,1:T(8,128)(2,1)S(1)} %get-tuple-element.518) | copy-start | bytes 1572868 | tf_op jit(solution)/shard_map/while
  62.0 3.7 %copy-start.1 = (bf16[128,16,128]{2,0,1:T(8,128)(2,1)S(1)}, bf16[128,16,128]{2,0,1:T(8,128)(2,1)}, u32[]{:S(2)}) copy-start(bf16[128,16,128]{2,0,1:T(8,128)(2,1)} %copy-done) | copy-start | bytes 1572868 | tf_op jit(solution)/shard_map/while
  65.8 197.3 %reduce-scatter.5.cloned.1.call-start = ((), (), s32[]{:S(2)}) async-start(), calls=%async_computation.4 | async-start | bytes 540672 | tf_op jit(solution)/shard_map/reduce_scatter | solution.py:106
  113.5 10.9 %copy-start.7 = (bf16[128,16,128]{2,1,0:T(8,128)(2,1)S(1)}, bf16[128,16,128]{2,1,0:T(8,128)(2,1)}, u32[]{:S(2)}) copy-start(bf16[128,16,128]{2,1,0:T(8,128)(2,1)} %param.15) | copy-start | bytes 1572868
  113.5 1.3 copy-start.4
  113.6 2.5 copy-start.2
  116.1 1.0 copy-start.5
  117.1 1.9 copy-start.3
  119.0 1.3 copy-start.4
  119.0 2.5 copy-start.2
  121.5 1.0 copy-start.5
  122.5 1.9 copy-start.3
  124.4 4.4 %copy-start.6 = (f32[128,16,128]{2,0,1:T(8,128)S(1)}, f32[128,16,128]{2,0,1:T(8,128)}, u32[]{:S(2)}) copy-start(f32[128,16,128]{2,0,1:T(8,128)} %get-tuple-element.344) | copy-start | bytes 3145732
Sparse Core Ops, SparseCore 0:
  9.9 26.7 all-gather.1
  65.9 27.2 reduce-scatter.2
  128.9 134.0 reduce-scatter.4
where the time goes:
time: 270 us
  waiting for transfers between devices  176 us (65%)
  blocking collectives  25.5 us (9%)
  matrix products  25.3 us (9%)
  local copies, waits for them, and re-layouts  16.9 us (6%)
  between operations  13.8 us (5%)
  other arithmetic  11.4 us (4%)
    reduce_scatter x1, waiting for transfers between devices, per_device(): lax.psum_scatter(jnp.einsum('tjs,tjd->sd', coefficient, indexer_query, pr...  133 us
    reduce_scatter x1, waiting for transfers between devices, per_device(): lax.psum_scatter(tile_sums, 'head', scatter_dimension=1, tiled=True)  27.1 us
    all_gather x1, waiting for transfers between devices, per_device(): lax.all_gather(key_latent, 'ctx', axis=0, tiled=True)  15.8 us
    all_gather x1, blocking collectives, per_device(): grad_logit = lax.all_gather(share_grad, 'head', axis=0, tiled=True)  14.5 us
    dot_general x2, matrix products, forward(): jnp.einsum('thl,sl->ths', query_latent, latent_block, preferred_element_t...  13.6 us
    all_gather x1, blocking collectives, per_device(): lax.all_gather(indexer_key, 'ctx', axis=0, tiled=True)  11 us
    dynamic_update_slice x2, other arithmetic, forward(): positive = lax.dynamic_update_slice_in_dim(positive, idx_dot > 0, offset, 2)  5.67 us
  transfers between devices with their start and end apart: 3, of which 3 were waited for; matrix products, arithmetic and copies ran while one was open for 1% of the time, Pallas kernels for 0%

commit v1 on v0

--- a/solution.py
+++ b/solution.py
@@ -78,7 +78,21 @@
         query_pos, lax.axis_index("head") * share_count, share_count, 0
     )
     share_grad = gradient(share_sums, share_pos, key_pos)
-    grad_logit = lax.all_gather(share_grad, "head", axis=0, tiled=True)
+    w_in = share_grad
+    part_now = lax.psum(1, axis_name="head")
+    low = lax.axis_index("head")
+    o_now, state_now, far_arr = (part_now, low, w_in.shape[0])
+    steps_seen = tuple(
+        (dev_j * o_now if idx == 0 else dev_j for idx, dev_j in enumerate(w_in.shape))
+    )
+    z = jnp.zeros(steps_seen, w_in.dtype)
+    grad_logit = lax.dynamic_update_slice_in_dim(z, w_in, state_now * far_arr, axis=0)
+    for d in range(1, o_now):
+        z1 = tuple(((idx, (idx + 1) % o_now) for idx in range(o_now)))
+        w_in = lax.ppermute(w_in, axis_name="head", perm=z1)
+        grad_logit = lax.dynamic_update_slice_in_dim(
+            grad_logit, w_in, (state_now - d) % o_now * far_arr, axis=0
+        )
     weight_scaled = weight_float * idx_scale
 
     def backward(step_index, state):

time: 270 us -> 274 us (1.015)
  waiting for transfers between devices: 176 us -> 195 us
  blocking collectives: 25.5 us -> 11 us
    ppermute x0 -> x3, waiting for transfers between devices: none -> 18 us  [per_device(): w_in = lax.ppermute(w_in, axis_name='head', perm=z1)]
    all_gather x1 -> x0, blocking collectives: 14.5 us -> none  [per_device(): grad_logit = lax.all_gather(share_grad, 'head', axis=0, tiled=True)]
  transfers between devices with their start and end apart: 3 -> 6, of which waited for: 3 -> 6; matrix products, arithmetic and copies ran while one was open for 1% -> 1% of each run, Pallas kernels for 0% -> 0%
where the time goes in v1:
time: 274 us
  waiting for transfers between devices  195 us (71%)
  matrix products  25.3 us (9%)
  local copies, waits for them, and re-layouts  16.8 us (6%)
  between operations  14 us (5%)
  other arithmetic  11.4 us (4%)
  blocking collectives  11 us (4%)
    reduce_scatter x1, waiting for transfers between devices, per_device(): lax.psum_scatter(jnp.einsum('tjs,tjd->sd', coefficient, indexer_query, pr...  133 us
    reduce_scatter x1, waiting for transfers between devices, per_device(): lax.psum_scatter(tile_sums, 'head', scatter_dimension=1, tiled=True)  27.1 us
    ppermute x3, waiting for transfers between devices, per_device(): w_in = lax.ppermute(w_in, axis_name='head', perm=z1)  18 us
    all_gather x1, waiting for transfers between devices, per_device(): lax.all_gather(key_latent, 'ctx', axis=0, tiled=True)  15.8 us
    dot_general x2, matrix products, forward(): jnp.einsum('thl,sl->ths', query_latent, latent_block, preferred_element_t...  13.6 us
    all_gather x1, blocking collectives, per_device(): lax.all_gather(indexer_key, 'ctx', axis=0, tiled=True)  11 us
    dynamic_update_slice x2, other arithmetic, forward(): positive = lax.dynamic_update_slice_in_dim(positive, idx_dot > 0, offset, 2)  5.67 us
  transfers between devices with their start and end apart: 6, of which 6 were waited for; matrix products, arithmetic and copies ran while one was open for 1% of the time, Pallas kernels for 0%

profile of v1, /device:TPU:0, one launch (start us, length us, event | category | flops | bytes accessed | tf_op | source)
XLA Modules:
  0.0 273.6 jit_solution(5447429482198100509)
XLA Ops:
  7.2 0.0 all-gather.2.cloned.1.call-start
  7.2 0.7 all-gather.2.cloned.1.call-update
  7.9 0.0 reduce-scatter.3.cloned.1.call-start
  8.0 0.7 convert_element_type.20
  8.6 1.2 copy.14
  9.8 11.0 %all_gather.7 = bf16[1024,128]{1,0:T(8,128)(2,1)S(1)} all-gather(bf16[128,128]{1,0:T(8,128)(2,1)} %param.16), channel_id=1, replica_groups=mesh['ctx'=8,'head'=4] {'ctx'}, dimensions={0}, use_global_device_ids=true | all-gather | bytes 294912 | tf_op jit(solution)/shard_map/all_gather | solution.py:40
  20.8 15.8 %all-gather.2.cloned.1.call-done = bf16[1024,576]{0,1:T(8,128)(2,1)} async-done(((bf16[128,576]{0,1:T(8,128)(2,1)}), bf16[1024,576]{0,1:T(8,128)(2,1)}) %all-gather.2.cloned.1.call-update) | async-done | bytes 1179664 | tf_op jit(solution)/shard_map/all_gather | solution.py:39
  36.7 1.1 broadcast_in_dim.52.clone
  37.8 0.8 broadcast_in_dim.53
  38.6 0.0 copy-done.9
  38.6 0.0 copy-start.10
  38.6 0.0 copy-start.8
  38.6 27.0 %while.31 = (s32[]{:T(128)}, f32[2,128,1024]{2,1,0:T(8,128)}, pred[128,16,1024]{0,2,1:T(32,128)(4,1)S(1)}, bf16[1024,576]{0,1:T(8,128)(2,1)}, bf16[128,32,576]{0...) while((s32[]{:T(128)}, f32[2,128,1024]{2,1,0:T(8,128)}, ...), condition=%wide.region_3.0_spmd, body=%wide.region_0.0_spmd.sunk | while | flops 2694905856 | bytes 23814388 | solution.py:74
  38.6 6.8 %exponential_reduce_fusion.2 = f32[512,128]{1,0:T(8,128)S(1)} fusion(f32[128,32]{0,1:T(8,128)S(1)} %get-tuple-element.517, bf16[128,32,576]{0,2,1:T(8,128)(2,1)} %get-tuple-element.516, bf16[1024,576]{0,1:T(8,128)(2,1)} %get-tuple-element.515, s32[]{:T(128)S(6)} %select_n.121), kind=kOutput, calls=%fused_computation.clone.1 | convolution fusion | flops 2422145024 | bytes 5586948 | tf_op jit(solution)/shard_map/while/body/eval_jaxpr/thl,sl->ths/dot_general | solution.py:52
  45.4 0.0 copy-done
  45.4 2.7 multiply_reduce_fusion.2
  48.1 0.1 pad_maximum_fusion.2
  48.2 0.2 copy.30
  48.4 0.0 copy-start.1
  48.4 0.8 constant_dynamic-update-slice_fusion.6
  49.2 2.8 %bitcast_dynamic-update-slice_fusion.2 = pred[128,16,1024]{0,2,1:T(32,128)(4,1)S(1)} fusion(pred[128,16,1024]{0,2,1:T(32,128)(4,1)S(1)} %get-tuple-element.501, s32[]{:T(128)S(6)} %select_n.121, f32[512,128,16]{1,0,2:T(8,128)} %get-tuple-element.478), kind=kLoop, calls=%fused_computation.2.clone.1 | loop fusion | flops 1048576 | bytes 5242884 | tf_op jit(solution)/shard_map/while/body/eval_jaxpr/dynamic_update_slice | solution.py:67
  52.1 6.8 %exponential_reduce_fusion.2 = f32[512,128]{1,0:T(8,128)S(1)} fusion(f32[128,32]{0,1:T(8,128)S(1)} %get-tuple-element.517, bf16[128,32,576]{0,2,1:T(8,128)(2,1)} %get-tuple-element.516, bf16[1024,576]{0,1:T(8,128)(2,1)} %get-tuple-element.515, s32[]{:T(128)S(6)} %select_n.121), kind=kOutput, calls=%fused_computation.clone.1 | convolution fusion | flops 2422145024 | bytes 5586948 | tf_op jit(solution)/shard_map/while/body/eval_jaxpr/thl,sl->ths/dot_general | solution.py:52
  58.9 0.0 copy-done
  58.9 2.7 multiply_reduce_fusion.2
  61.6 0.1 pad_maximum_fusion.2
  61.7 0.2 copy.30
  61.9 0.8 constant_dynamic-update-slice_fusion.6
  62.7 2.8 %bitcast_dynamic-update-slice_fusion.2 = pred[128,16,1024]{0,2,1:T(32,128)(4,1)S(1)} fusion(pred[128,16,1024]{0,2,1:T(32,128)(4,1)S(1)} %get-tuple-element.501, s32[]{:T(128)S(6)} %select_n.121, f32[512,128,16]{1,0,2:T(8,128)} %get-tuple-element.478), kind=kLoop, calls=%fused_computation.2.clone.1 | loop fusion | flops 1048576 | bytes 5242884 | tf_op jit(solution)/shard_map/while/body/eval_jaxpr/dynamic_update_slice | solution.py:67
  65.6 0.0 reduce-scatter.3.cloned.1.call-update
  65.6 0.0 reduce-scatter.5.cloned.1.call-start
  65.7 0.1 iota_add_fusion
  65.8 0.1 add.117
  65.9 0.1 dynamic_slice.42
  65.9 27.1 %reduce-scatter.3.cloned.1.call-done = f32[2,32,1024]{2,1,0:T(8,128)} async-done(((f32[2,128,1024]{2,1,0:T(8,128)}), f32[2,32,1024]{2,1,0:T(8,128)}) %reduce-scatter.3.cloned.1.call-update) | async-done | bytes 262160 | tf_op jit(solution)/shard_map/reduce_scatter | solution.py:75
  93.1 1.1 fusion.17
  94.2 1.2 fusion.20
  95.4 1.1 constant_dynamic-update-slice_fusion.4
  96.5 0.1 collective-permute-start
  96.7 5.9 %collective-permute-done = bf16[32,1024]{1,0:T(8,128)(2,1)S(1)} collective-permute-done((bf16[32,1024]{1,0:T(8,128)(2,1)S(1)}, bf16[32,1024]{1,0:T(8,128)(2,1)S(1)}, u32[]{:S(2)}, u32[]{:S(2)}) %collective-permute-start) | collective-permute-done | bytes 65568 | tf_op jit(solution)/shard_map/ppermute | solution.py:92
  102.6 0.0 collective-permute-start.1
  102.6 6.0 %collective-permute-done.1 = bf16[32,1024]{1,0:T(8,128)(2,1)S(1)} collective-permute-done((bf16[32,1024]{1,0:T(8,128)(2,1)S(1)}, bf16[32,1024]{1,0:T(8,128)(2,1)S(1)}, u32[]{:S(2)}, u32[]{:S(2)}) %collective-permute-start.1) | collective-permute-done | bytes 65568 | tf_op jit(solution)/shard_map/ppermute | solution.py:92
  108.7 0.0 collective-permute-start.2
  108.7 6.0 %collective-permute-done.2 = bf16[32,1024]{1,0:T(8,128)(2,1)S(1)} collective-permute-done((bf16[32,1024]{1,0:T(8,128)(2,1)S(1)}, bf16[32,1024]{1,0:T(8,128)(2,1)S(1)}, u32[]{:S(2)}, u32[]{:S(2)}) %collective-permute-start.2) | collective-permute-done | bytes 65568 | tf_op jit(solution)/shard_map/ppermute | solution.py:92
  114.7 2.5 broadcast_in_dim.50
  117.2 10.9 %while.32 = (s32[]{:T(128)}, bf16[128,16,1024]{2,0,1:T(8,128)(2,1)}, f32[128,16,128]{2,0,1:T(8,128)}, pred[128,16,1024]{0,2,1:T(32,128)(4,1)S(1)}, bf16[128,1024...) while((s32[]{:T(128)}, ...), condition=%wide.region_9.10_spmd.clone, body=%wide.region_8.9_spmd.clone.sunk | while | flops 275316736 | bytes 53494056 | solution.py:119
  117.3 0.1 constant_dynamic-slice_fusion.2
  117.3 1.2 copy.31
  118.6 1.0 fusion.37
  119.6 0.2 copy-done.2
  119.8 0.7 fusion.36
  120.5 0.3 copy-done.5
  120.8 1.9 copy-done.3
  122.7 0.1 constant_dynamic-slice_fusion.2
  122.8 1.2 copy.31
  124.0 1.0 fusion.37
  125.1 0.1 copy-done.2
  125.2 0.7 fusion.36
  125.9 0.3 copy-done.5
  126.2 1.9 copy-done.3
  128.1 0.0 copy-done.7
  128.1 4.4 %convolution_bitcast_fusion = f32[1024,128]{1,0:T(8,128)} fusion(bf16[128,16,1024]{2,0,1:T(8,128)(2,1)} %get-tuple-element.285, bf16[128,16,128]{2,1,0:T(8,128)(2,1)S(1)} %copy-done.7), kind=kOutput, calls=%fused_computation.26 | convolution fusion | flops 536870912 | bytes 5242880 | tf_op jit(solution)/shard_map/tjs,tjd->sd/dot_general | solution.py:121
  132.5 0.0 reduce-scatter.5.cloned.1.call-update
  132.5 1.6 copy.19
  134.1 132.9 %reduce-scatter.5.cloned.1.call-done = f32[32,128]{1,0:T(8,128)} async-done(((f32[1024,128]{1,0:T(8,128)}), f32[32,128]{1,0:T(8,128)}) %reduce-scatter.5.cloned.1.call-update) | async-done | bytes 16400 | tf_op jit(solution)/shard_map/reduce_scatter | solution.py:120
  (32 shorter events, 0.2 us)
Async XLA Ops:
  7.2 31.4 %copy-start.9 = (f32[128,32]{0,1:T(8,128)S(1)}, f32[128,32]{0,1:T(8,128)}, u32[]{:S(2)}) copy-start(f32[128,32]{0,1:T(8,128)} %param.14) | copy-start | bytes 49156
  7.2 29.5 %all-gather.2.cloned.1.call-start = ((), (), s32[]{:S(2)}) async-start(), calls=%async_computation.2 | async-start | bytes 1327104 | tf_op jit(solution)/shard_map/all_gather | solution.py:39
  7.9 85.2 %reduce-scatter.3.cloned.1.call-start = ((), (), s32[]{:S(2)}) async-start(), calls=%async_computation.3 | async-start | bytes 1310720 | tf_op jit(solution)/shard_map/reduce_scatter | solution.py:75
  38.6 27.1 %copy-start.10 = (s32[16]{0:T(128)S(1)}, s32[16]{0:T(128)}, u32[]{:S(2)}) copy-start(s32[16]{0:T(128)} %param.11) | copy-start | bytes 196
  38.6 58.0 %copy-start.8 = (bf16[128,16]{0,1:T(8,128)(2,1)S(1)}, bf16[128,16]{0,1:T(8,128)(2,1)}, u32[]{:S(2)}) copy-start(bf16[128,16]{0,1:T(8,128)(2,1)} %param.17) | copy-start | bytes 12292
  38.6 6.8 %copy-start = (bf16[128,16,128]{2,0,1:T(8,128)(2,1)}, bf16[128,16,128]{2,0,1:T(8,128)(2,1)S(1)}, u32[]{:S(2)}) copy-start(bf16[128,16,128]{2,0,1:T(8,128)(2,1)S(1)} %get-tuple-element.520) | copy-start | bytes 1572868 | tf_op jit(solution)/shard_map/while
  48.4 3.7 %copy-start.1 = (bf16[128,16,128]{2,0,1:T(8,128)(2,1)S(1)}, bf16[128,16,128]{2,0,1:T(8,128)(2,1)}, u32[]{:S(2)}) copy-start(bf16[128,16,128]{2,0,1:T(8,128)(2,1)} %copy-done) | copy-start | bytes 1572868 | tf_op jit(solution)/shard_map/while
  52.1 6.8 %copy-start = (bf16[128,16,128]{2,0,1:T(8,128)(2,1)}, bf16[128,16,128]{2,0,1:T(8,128)(2,1)S(1)}, u32[]{:S(2)}) copy-start(bf16[128,16,128]{2,0,1:T(8,128)(2,1)S(1)} %get-tuple-element.520) | copy-start | bytes 1572868 | tf_op jit(solution)/shard_map/while
  61.9 3.7 %copy-start.1 = (bf16[128,16,128]{2,0,1:T(8,128)(2,1)S(1)}, bf16[128,16,128]{2,0,1:T(8,128)(2,1)}, u32[]{:S(2)}) copy-start(bf16[128,16,128]{2,0,1:T(8,128)(2,1)} %copy-done) | copy-start | bytes 1572868 | tf_op jit(solution)/shard_map/while
  65.6 201.4 %reduce-scatter.5.cloned.1.call-start = ((), (), s32[]{:S(2)}) async-start(), calls=%async_computation.4 | async-start | bytes 540672 | tf_op jit(solution)/shard_map/reduce_scatter | solution.py:120
  96.5 6.1 %collective-permute-start = (bf16[32,1024]{1,0:T(8,128)(2,1)S(1)}, bf16[32,1024]{1,0:T(8,128)(2,1)S(1)}, u32[]{:S(2)}, u32[]{:S(2)}) collective-permute-start(bf16[32,1024]{1,0:T(8,128)(2,1)S(1)} %get-tuple-element.381), channel_id=1, source_target_pairs={{0,1},{1,2},{2,3},{3,0},{4,5},{5,6},{6,7},{7,4},{8,9},{9,10},{10,1... | collective-permute-start | bytes 196616 | tf_op jit(solution)/shard_map/ppermute | solution.py:92
  102.6 6.1 %collective-permute-start.1 = (bf16[32,1024]{1,0:T(8,128)(2,1)S(1)}, bf16[32,1024]{1,0:T(8,128)(2,1)S(1)}, u32[]{:S(2)}, u32[]{:S(2)}) collective-permute-start(bf16[32,1024]{1,0:T(8,128)(2,1)S(1)} %collective-permute-done), channel_id=1, source_target_pairs={{0,1},{1,2},{2,3},{3,0},{4,5},{5,6},{6,7},{7,4},{8,9},{9,10},{10,1... | collective-permute-start | bytes 196616 | tf_op jit(solution)/shard_map/ppermute | solution.py:92
  108.7 6.1 %collective-permute-start.2 = (bf16[32,1024]{1,0:T(8,128)(2,1)S(1)}, bf16[32,1024]{1,0:T(8,128)(2,1)S(1)}, u32[]{:S(2)}, u32[]{:S(2)}) collective-permute-start(bf16[32,1024]{1,0:T(8,128)(2,1)S(1)} %collective-permute-done.1), channel_id=1, source_target_pairs={{0,1},{1,2},{2,3},{3,0},{4,5},{5,6},{6,7},{7,4},{8,9},{9,10},{10,1... | collective-permute-start | bytes 196616 | tf_op jit(solution)/shard_map/ppermute | solution.py:92
  117.2 10.9 %copy-start.7 = (bf16[128,16,128]{2,1,0:T(8,128)(2,1)S(1)}, bf16[128,16,128]{2,1,0:T(8,128)(2,1)}, u32[]{:S(2)}) copy-start(bf16[128,16,128]{2,1,0:T(8,128)(2,1)} %param.15) | copy-start | bytes 1572868
  117.2 1.3 copy-start.4
  117.2 2.5 copy-start.2
  119.8 1.0 copy-start.5
  120.8 1.9 copy-start.3
  122.7 1.3 copy-start.4
  122.7 2.5 copy-start.2
  125.2 1.0 copy-start.5
  126.2 1.9 copy-start.3
  128.1 4.4 %copy-start.6 = (f32[128,16,128]{2,0,1:T(8,128)S(1)}, f32[128,16,128]{2,0,1:T(8,128)}, u32[]{:S(2)}) copy-start(f32[128,16,128]{2,0,1:T(8,128)} %get-tuple-element.344) | copy-start | bytes 3145732
Sparse Core Ops, SparseCore 0:
  9.9 26.7 all-gather.1
  65.8 27.2 reduce-scatter.2
  132.6 134.3 reduce-scatter.4
